TPU v7x, 32 devices: a whole 2x2x4 slice. The times are simulated.
32 devices in a mesh: tm: 2 (over x), lat: 4 (over y, core), lon: 4 (over z).
Axes of the slice: x: 2, y: 2, z: 4, core: 2. Of those that a mesh axis runs over, the one named last changes fastest.
Arguments:
- control: float32 [16, 8, 64, 512], P(None, None, 'lat', 'lon'), may hold values from -6 to 6
- ens_pert: bfloat16 [2, 16, 8, 64, 512], P('tm', None, None, 'lat', 'lon'), may hold values from -6 to 6
- lat_filter: bfloat16 [64, 64], replicated, may hold values from 0 to 2.5, as said below
- lon_filter: bfloat16 [512, 512], replicated, may hold values from 0 to 2.5, as said below
- interp_lat: float32 [128, 18], P('lat'), may hold values from -1.5 to 1.5
- interp_lon: float32 [1024, 130], P('lon'), may hold values from -0.5 to 0.5
- obs_cell: int32 [2, 2, 4, 4, 64], P('tm', None, 'lat', 'lon'), may hold values from 0 to 65535
- obs_count: int32 [2, 2, 4, 4], P('tm', None, 'lat', 'lon'), may hold values from 1 to 64, as said below
- obs_value: float32 [2, 2, 4, 4, 64], P('tm', None, 'lat', 'lon'), may hold values from -18 to 18
- obs_weight: float32 [2, 2, 4, 4, 64], P('tm', None, 'lat', 'lon'), may hold values from 0.1 to 0.4
Outputs:
- gradient: float32 [16, 8, 64, 512], P(None, None, 'lat', 'lon')
Inputs may be any that keep to these rules, and one draw needn't show every extreme that they name: `lat_filter`: within the latitude spreading matrix all entries are non-negative. `lon_filter`: entries are non-negative. `obs_count`: each count is at least 1 and at most 64; in every draw some count equals 64.
All inputs are finite; a program needn't handle non-finite values.
Results may differ from a plain program's by a relative error of at most 0.0003.
Values sent between devices are 32-bit elements; how exact they have to be, the bound alone decides.
No kernel may reach another device: no remote copies, remote signals or barrier semaphores. Data moves between devices by JAX's collectives and lax.ppermute only.
A program may use at most 64 MiB of HBM per device.

v0:
```python
import jax
import jax.numpy as jnp
from jax import lax
from jax.sharding import PartitionSpec as P

HIGHEST = lax.Precision.HIGHEST
DIRECTIONS = ((-1, -1), (-1, 0), (-1, 1), (0, -1), (0, 1), (1, -1), (1, 0), (1, 1))


def extended(array, sides, width):
    for axis, dim in sides:
        size, length = (lax.axis_size(axis), array.shape[dim])
        up = [(i, (i + 1) % size) for i in range(size)]
        down = [(j, i) for i, j in up]
        last = lax.slice_in_dim(array, length - width, length, axis=dim)
        first = lax.slice_in_dim(array, 0, width, axis=dim)
        before = lax.ppermute(last, axis, up)
        after = lax.ppermute(first, axis, down)
        array = jnp.concatenate([before, array, after], axis=dim)
    return array


def spread_field(source, lat_matrix, lon_matrix):
    members, levels, lat_rows, lon_cols = source.shape
    fields = members * levels
    stacked = source.reshape(fields, lat_rows, lon_cols)
    across = jnp.einsum(
        "ab,mbk->mak",
        lat_matrix,
        lax.all_to_all(stacked, "lat", split_axis=0, concat_axis=1, tiled=True),
        precision=HIGHEST,
    )
    halfway = lax.all_to_all(across, "lat", split_axis=1, concat_axis=0, tiled=True)
    column = lax.axis_index("lon") * lon_cols
    portion = lax.all_gather(halfway, "lon", axis=2, tiled=True)
    section = lax.dynamic_slice(lon_matrix, (column, 0), (lon_cols, portion.shape[2]))
    result = jnp.einsum("mak,ck->mac", portion, section, precision=HIGHEST)
    return result.reshape(members, levels, lat_rows, lon_cols)


def rim_region(offset, length):
    if offset < 0:
        return slice(0, 1)
    if offset > 0:
        return slice(length + 1, length + 2)
    return slice(1, length + 1)


def own_cells(offset, length):
    if offset < 0:
        return slice(0, 1)
    if offset > 0:
        return slice(length - 1, length)
    return slice(0, length)


def per_device(
    control,
    ens_pert,
    lat_filter,
    lon_filter,
    interp_lat,
    interp_lon,
    obs_cell,
    obs_count,
    obs_value,
    obs_weight,
):
    lat_matrix = lat_filter.astype(jnp.float32)
    lon_matrix = lon_filter.astype(jnp.float32)
    members = control.shape[0]
    slot_pert = ens_pert[0]
    share = members // lax.axis_size("tm")
    first = lax.axis_index("tm") * share
    mine = lax.dynamic_slice_in_dim(control, first, share, 0)
    spread_mine = spread_field(mine, lat_matrix, lon_matrix)
    weights_here = slot_pert.astype(jnp.float32)
    increment = jnp.sum(
        lax.all_gather(spread_mine, "tm", axis=0, tiled=True) * weights_here, axis=0
    )
    levels, lat_rows, lon_cols = increment.shape
    padded = extended(increment, (("lat", 1), ("lon", 2)), 1)
    lat_band = lax.axis_index("lat")
    edge_rows = jnp.arange(lat_rows + 2)
    dropped = (edge_rows == 0) & (lat_band == 0) | (edge_rows == lat_rows + 1) & (
        lat_band == lax.axis_size("lat") - 1
    )
    keeping = jnp.logical_not(dropped).astype(jnp.float32)[None, :, None]
    padded = padded * keeping
    rowwise = jnp.einsum("ip,lpq->liq", interp_lat, padded, precision=HIGHEST)
    finer = jnp.einsum("liq,jq->lij", rowwise, interp_lon, precision=HIGHEST)
    fine_rows = finer.shape[1]
    fine_cols = finer.shape[2]
    flat_field = finer.reshape(-1)
    slots_range = jnp.arange(obs_cell.shape[-1])
    usable = (slots_range < obs_count[..., None]).astype(jnp.float32)
    package = jnp.stack([obs_cell.astype(jnp.float32), obs_value, obs_weight * usable], axis=0)
    arrived = lax.all_to_all(package, "tm", split_axis=2, concat_axis=1, tiled=True)
    places = arrived[0].reshape(-1).astype(jnp.int32)
    targets = arrived[1].reshape(-1)
    weights = arrived[2].reshape(-1)
    seen = flat_field[places]
    departure = weights * (seen - targets)
    fine_grad = jnp.zeros_like(flat_field).at[places].add(departure)
    fine_grad = fine_grad.reshape(levels, fine_rows, fine_cols)
    pulled = jnp.einsum("jq,lij->liq", interp_lon, fine_grad, precision=HIGHEST)
    coarse_pad = jnp.einsum("ip,liq->lpq", interp_lat, pulled, precision=HIGHEST) * keeping
    outgoing = []
    for lat_step, lon_step in DIRECTIONS:
        holder = jnp.zeros((levels, lat_rows, lon_cols), jnp.float32)
        holder = holder.at[:, own_cells(lat_step, lat_rows), own_cells(lon_step, lon_cols)].set(
            coarse_pad[:, rim_region(lat_step, lat_rows), rim_region(lon_step, lon_cols)]
        )
        outgoing.append(holder)
    bundle = jnp.stack(outgoing, axis=0)
    incoming = extended(bundle, (("lat", 2), ("lon", 3)), 1)
    coarse_grad = coarse_pad[:, 1:-1, 1:-1]
    for number, (lat_step, lon_step) in enumerate(DIRECTIONS):
        coarse_grad = coarse_grad.at[
            :, own_cells(-lat_step, lat_rows), own_cells(-lon_step, lon_cols)
        ].add(incoming[number][:, rim_region(-lat_step, lat_rows), rim_region(-lon_step, lon_cols)])
    weights_here = slot_pert.astype(jnp.float32)
    share_grad = lax.psum_scatter(
        weights_here * coarse_grad[None], "tm", scatter_dimension=0, tiled=True
    )
    adjoint_mine = spread_field(share_grad, lat_matrix.T, lon_matrix.T)
    return control + lax.all_gather(adjoint_mine, "tm", axis=0, tiled=True)


def solution(mesh):
    placed = (
        P(None, None, "lat", "lon"),
        P("tm", None, None, "lat", "lon"),
        P(),
        P(),
        P("lat", None),
        P("lon", None),
        P("tm", None, "lat", "lon", None),
        P("tm", None, "lat", "lon"),
        P("tm", None, "lat", "lon", None),
        P("tm", None, "lat", "lon", None),
    )
    return jax.shard_map(
        per_device,
        mesh=mesh,
        in_specs=placed,
        out_specs=P(None, None, "lat", "lon"),
        check_vma=False,
    )
```

profile of v0, /device:TPU:0, one launch (start us, length us, event | category | flops | bytes accessed | tf_op | source)
XLA Modules:
  0.0 265.9 jit_solution(17152153929202696150)
XLA Ops:
  7.7 12.9 %all_to_all.81 = f32[64,16,128]{2,1,0:T(8,128)S(1)} all-to-all(f32[64,16,128]{2,1,0:T(8,128)S(1)} %bitcast.107), channel_id=1, replica_groups=mesh['tm'=2,'lat'=4,'lon'=4] {'lat'}, dimensions={0} | all-to-all | bytes 1048576 | tf_op jit(solution)/shard_map/all_to_all | solution.py:30
  21.4 11.2 %all_to_all.82 = f32[16,64,128]{2,0,1:T(8,128)S(1)} all-to-all(f32[16,64,128]{2,0,1:T(8,128)S(1)} %copy.43), channel_id=1, replica_groups=mesh['tm'=2,'lat'=4,'lon'=4] {'lat'}, dimensions={1} | all-to-all | bytes 1048576 | tf_op jit(solution)/shard_map/all_to_all | solution.py:33
  33.7 46.6 %all-gather.5.cloned.1.call-done = f32[64,16,512]{2,1,0:T(8,128)} async-done(((f32[64,16,128]{2,1,0:T(8,128)}), f32[64,16,512]{2,1,0:T(8,128)}) %all-gather.5.cloned.1.call-update) | async-done | bytes 2097168 | tf_op jit(solution)/shard_map/all_gather | solution.py:35
  80.3 3.4 %fusion.16 = f32[64,16,128]{2,1,0:T(8,128)} fusion(f32[64,16,512]{2,1,0:T(8,128)} %all-gather.5.cloned.1.call-done, bf16[512,512]{1,0:T(8,128)(2,1)S(1)} %copy-done, s32[]{:T(128)S(6)} %select_n.20), kind=kOutput, calls=%fused_computation.35 | convolution fusion | flops 805306368 | bytes 2752516 | tf_op jit(solution)/shard_map/mak,ck->mac/dot_general | solution.py:37
  85.7 3.2 %all-to-all-start = ((f32[2,1,192]{2,1,0:T(1,128)}), f32[2,1,192]{2,1,0:T(1,128)S(1)}, u32[]{:S(2)}, u32[]{:S(2)}) async-start(f32[2,1,192]{2,1,0:T(1,128)} %reshape.675), calls=%async_computation | async-start | bytes 4096 | tf_op jit(solution)/shard_map/all_to_all | solution.py:98
  90.4 2.2 all-to-all-done
  93.5 9.9 %all-gather.7.cloned.1.call-done = f32[16,8,16,128]{3,2,1,0:T(8,128)} async-done(((f32[8,8,16,128]{3,2,1,0:T(8,128)}), f32[16,8,16,128]{3,2,1,0:T(8,128)}) %all-gather.7.cloned.1.call-update) | async-done | bytes 1048592 | tf_op jit(solution)/shard_map/all_gather | solution.py:79
  104.9 1.7 collective-permute-start.1
  108.0 1.5 collective-permute-start.2
  109.5 2.4 collective-permute-start.3
  112.1 3.1 %collective-permute-done.2 = f32[8,18,1]{2,1,0:T(8,128)S(1)} collective-permute-done((f32[8,18,1]{2,1,0:T(8,128)S(1)}, f32[8,18,1]{2,1,0:T(8,128)S(1)}, u32[]{:S(2)}, u32[]{:S(2)}) %collective-permute-start.2) | collective-permute-done | bytes 608 | tf_op jit(solution)/shard_map/ppermute | solution.py:17
  115.1 1.8 collective-permute-done.3
  124.5 1.6 collective-permute-start.5
  126.1 1.6 collective-permute-done.4
  130.2 2.6 collective-permute-start.7
  138.0 2.1 add_select_fusion
  140.1 1.4 scatter-add.44
  142.8 20.4 %reduce-scatter.2.cloned.1.call-done = f32[8,8,16,128]{3,2,1,0:T(8,128)} async-done(((f32[16,8,16,128]{3,2,1,0:T(8,128)}), f32[8,8,16,128]{3,2,1,0:T(8,128)}) %reduce-scatter.2.cloned.1.call-update) | async-done | bytes 524304 | tf_op jit(solution)/shard_map/reduce_scatter | solution.py:123
  163.2 12.3 %all_to_all.83 = f32[64,16,128]{2,1,0:T(8,128)S(1)} all-to-all(f32[64,16,128]{2,1,0:T(8,128)} %bitcast.117), channel_id=1, replica_groups=mesh['tm'=2,'lat'=4,'lon'=4] {'lat'}, dimensions={0} | all-to-all | bytes 1048576 | tf_op jit(solution)/shard_map/all_to_all | solution.py:30
  176.2 11.2 %all_to_all.84 = f32[16,64,128]{2,0,1:T(8,128)S(1)} all-to-all(f32[16,64,128]{2,0,1:T(8,128)S(1)} %copy.62), channel_id=1, replica_groups=mesh['tm'=2,'lat'=4,'lon'=4] {'lat'}, dimensions={1} | all-to-all | bytes 1048576 | tf_op jit(solution)/shard_map/all_to_all | solution.py:33
  188.5 45.4 %all-gather.9.cloned.1.call-done = f32[64,16,512]{2,1,0:T(8,128)} async-done(((f32[64,16,128]{2,1,0:T(8,128)}), f32[64,16,512]{2,1,0:T(8,128)}) %all-gather.9.cloned.1.call-update) | async-done | bytes 2097168 | tf_op jit(solution)/shard_map/all_gather | solution.py:35
  233.9 3.4 %fusion.14 = f32[64,16,128]{2,1,0:T(8,128)} fusion(f32[64,16,512]{2,1,0:T(8,128)} %all-gather.9.cloned.1.call-done, bf16[512,512]{1,0:T(8,128)(2,1)S(1)} %copy-done, s32[]{:T(128)S(6)} %select_n.20), kind=kOutput, calls=%fused_computation.33 | convolution fusion | flops 805306368 | bytes 2752516 | tf_op jit(solution)/shard_map/mak,ck->mac/dot_general | solution.py:37
  237.4 19.6 %all-gather.11.cloned.1.call-done = f32[16,8,16,128]{3,2,1,0:T(8,128)} async-done(((f32[8,8,16,128]{3,2,1,0:T(8,128)}), f32[16,8,16,128]{3,2,1,0:T(8,128)}) %all-gather.11.cloned.1.call-update) | async-done | bytes 1048592 | tf_op jit(solution)/shard_map/all_gather | solution.py:127
  257.0 2.3 add.122
  (125 shorter events, 28.3 us)
Async XLA Ops:
  6.5 73.7 %copy-start = (bf16[512,512]{1,0:T(8,128)(2,1)S(1)}, bf16[512,512]{1,0:T(8,128)(2,1)}, u32[]{:S(2)}) copy-start(bf16[512,512]{1,0:T(8,128)(2,1)} %param.45) | copy-start | bytes 1572868
  6.5 73.7 %all-gather.5.cloned.1.call-start = ((), (), s32[]{:S(2)}) async-start(), calls=%async_computation.6 | async-start | bytes 2621440 | tf_op jit(solution)/shard_map/all_gather | solution.py:35
  7.7 12.9 %copy-start.4 = (bf16[64,64]{1,0:T(8,128)(2,1)S(1)}, bf16[64,64]{1,0:T(8,128)(2,1)}, u32[]{:S(2)}) copy-start(bf16[64,64]{1,0:T(8,128)(2,1)} %param.44) | copy-start | bytes 24580
  33.6 69.9 %all-gather.7.cloned.1.call-start = ((), (), s32[]{:S(2)}) async-start(), calls=%async_computation.7 | async-start | bytes 1572864 | tf_op jit(solution)/shard_map/all_gather | solution.py:79
  33.6 50.1 %copy-start.7 = (f32[1,2,1,1,64]{4,3,2,1,0:T(1,128)S(1)}, f32[1,2,1,1,64]{4,3,2,1,0:T(1,128)}, u32[]{:S(2)}) copy-start(f32[1,2,1,1,64]{4,3,2,1,0:T(1,128)} %param.51) | copy-start | bytes 1540
  33.6 50.1 %copy-start.9 = (s32[1,2,1,1]{1,3,2,0:T(1,128)S(1)}, s32[1,2,1,1]{1,3,2,0:T(1,128)}, u32[]{:S(2)}) copy-start(s32[1,2,1,1]{1,3,2,0:T(1,128)} %param.49) | copy-start | bytes 28
  33.7 50.2 %copy-start.8 = (f32[1,2,1,1,64]{4,3,2,1,0:T(1,128)S(1)}, f32[1,2,1,1,64]{4,3,2,1,0:T(1,128)}, u32[]{:S(2)}) copy-start(f32[1,2,1,1,64]{4,3,2,1,0:T(1,128)} %param.50) | copy-start | bytes 1540
  33.7 56.0 %copy-start.10 = (s32[3]{0:T(128)S(1)}, s32[3]{0:T(128)}, u32[]{:S(2)}) copy-start(s32[3]{0:T(128)} %constant.430.clone.1) | copy-start | bytes 40
  33.7 69.7 %copy-start.2 = (bf16[1,16,8,16,128]{4,3,2,1,0:T(8,128)(2,1)S(1)}, bf16[1,16,8,16,128]{4,3,2,1,0:T(8,128)(2,1)}, u32[]{:S(2)}) copy-start(bf16[1,16,8,16,128]{4,3,2,1,0:T(8,128)(2,1)} %param.43) | copy-start | bytes 1572868
  83.7 33.2 %copy-start.5 = (f32[32,18]{0,1:T(8,128)S(1)}, f32[32,18]{0,1:T(8,128)}, u32[]{:S(2)}) copy-start(f32[32,18]{0,1:T(8,128)} %param.46) | copy-start | bytes 6916
  85.7 7.0 %all-to-all-start = ((f32[2,1,192]{2,1,0:T(1,128)}), f32[2,1,192]{2,1,0:T(1,128)S(1)}, u32[]{:S(2)}, u32[]{:S(2)}) async-start(f32[2,1,192]{2,1,0:T(1,128)} %reshape.675), calls=%async_computation | async-start | bytes 4096 | tf_op jit(solution)/shard_map/all_to_all | solution.py:98
  88.9 74.3 %reduce-scatter.2.cloned.1.call-start = ((), (), s32[]{:S(2)}) async-start(), calls=%async_computation.8 | async-start | bytes 1572864 | tf_op jit(solution)/shard_map/reduce_scatter | solution.py:123
  93.5 24.0 %copy-start.3 = (f32[256,130]{0,1:T(8,128)S(1)}, f32[256,130]{0,1:T(8,128)}, u32[]{:S(2)}) copy-start(f32[256,130]{0,1:T(8,128)} %param.47) | copy-start | bytes 399364
  104.8 3.1 %collective-permute-start = (f32[8,1,128]{2,1,0:T(1,128)S(1)}, f32[8,1,128]{2,1,0:T(1,128)S(1)}, u32[]{:S(2)}, u32[]{:S(2)}) collective-permute-start(f32[8,1,128]{2,1,0:T(1,128)S(1)} %get-tuple-element.222), channel_id=1, source_target_pairs={{0,4},{4,8},{8,12},{12,0},{1,5},{5,9},{9,13},{13,1},{2,6},{6,10},{... | collective-permute-start | bytes 12296 | tf_op jit(solution)/shard_map/ppermute | solution.py:17
  104.9 3.1 %collective-permute-start.1 = (f32[8,1,128]{2,1,0:T(1,128)S(1)}, f32[8,1,128]{2,1,0:T(1,128)S(1)}, u32[]{:S(2)}, u32[]{:S(2)}) collective-permute-start(f32[8,1,128]{2,1,0:T(1,128)S(1)} %get-tuple-element.223), channel_id=1, source_target_pairs={{4,0},{8,4},{12,8},{0,12},{5,1},{9,5},{13,9},{1,13},{6,2},{10,6},{... | collective-permute-start | bytes 12296 | tf_op jit(solution)/shard_map/ppermute | solution.py:18
  108.0 7.1 %collective-permute-start.2 = (f32[8,18,1]{2,1,0:T(8,128)S(1)}, f32[8,18,1]{2,1,0:T(8,128)S(1)}, u32[]{:S(2)}, u32[]{:S(2)}) collective-permute-start(f32[8,18,1]{2,1,0:T(8,128)S(1)} %get-tuple-element.220), channel_id=1, source_target_pairs={{0,1},{1,2},{2,3},{3,0},{4,5},{5,6},{6,7},{7,4},{8,9},{9,10},{10,1... | collective-permute-start | bytes 1736 | tf_op jit(solution)/shard_map/ppermute | solution.py:17
  109.5 7.5 %collective-permute-start.3 = (f32[8,18,1]{2,1,0:T(8,128)S(1)}, f32[8,18,1]{2,1,0:T(8,128)S(1)}, u32[]{:S(2)}, u32[]{:S(2)}) collective-permute-start(f32[8,18,1]{2,1,0:T(8,128)S(1)} %get-tuple-element.221), channel_id=1, source_target_pairs={{1,0},{2,1},{3,2},{0,3},{5,4},{6,5},{7,6},{4,7},{9,8},{10,9},{11,1... | collective-permute-start | bytes 1736 | tf_op jit(solution)/shard_map/ppermute | solution.py:18
  124.3 3.3 %collective-permute-start.4 = (f32[8,8,1,128]{3,1,2,0:T(8,128)S(1)}, f32[8,8,1,128]{3,1,2,0:T(8,128)S(1)}, u32[]{:S(2)}, u32[]{:S(2)}) collective-permute-start(f32[8,8,1,128]{3,1,2,0:T(8,128)S(1)} %get-tuple-element.211), channel_id=1, source_target_pairs={{0,4},{4,8},{8,12},{12,0},{1,5},{5,9},{9,13},{13,1},{2,6},{6,10},{... | collective-permute-start | bytes 98312 | tf_op jit(solution)/shard_map/ppermute | solution.py:17
  124.5 3.2 %collective-permute-start.5 = (f32[8,8,1,128]{3,1,2,0:T(8,128)S(1)}, f32[8,8,1,128]{3,1,2,0:T(8,128)S(1)}, u32[]{:S(2)}, u32[]{:S(2)}) collective-permute-start(f32[8,8,1,128]{3,1,2,0:T(8,128)S(1)} %get-tuple-element.212), channel_id=1, source_target_pairs={{4,0},{8,4},{12,8},{0,12},{5,1},{9,5},{13,9},{1,13},{6,2},{10,6},{... | collective-permute-start | bytes 98312 | tf_op jit(solution)/shard_map/ppermute | solution.py:18
  128.4 5.9 %collective-permute-start.6 = (f32[8,8,18,1]{2,1,3,0:T(8,128)S(1)}, f32[8,8,18,1]{2,1,3,0:T(8,128)S(1)}, u32[]{:S(2)}, u32[]{:S(2)}) collective-permute-start(f32[8,8,18,1]{2,1,3,0:T(8,128)S(1)} %copy.55), channel_id=1, source_target_pairs={{0,1},{1,2},{2,3},{3,0},{4,5},{5,6},{6,7},{7,4},{8,9},{9,10},{10,1... | collective-permute-start | bytes 13832 | tf_op jit(solution)/shard_map/ppermute | solution.py:17
  130.2 5.0 %collective-permute-start.7 = (f32[8,8,18,1]{2,1,3,0:T(8,128)S(1)}, f32[8,8,18,1]{2,1,3,0:T(8,128)S(1)}, u32[]{:S(2)}, u32[]{:S(2)}) collective-permute-start(f32[8,8,18,1]{2,1,3,0:T(8,128)S(1)} %copy.56), channel_id=1, source_target_pairs={{1,0},{2,1},{3,2},{0,3},{5,4},{6,5},{7,6},{4,7},{9,8},{10,9},{11,1... | collective-permute-start | bytes 13832 | tf_op jit(solution)/shard_map/ppermute | solution.py:18
  142.8 91.2 %all-gather.9.cloned.1.call-start = ((), (), s32[]{:S(2)}) async-start(), calls=%async_computation.9 | async-start | bytes 2621440 | tf_op jit(solution)/shard_map/all_gather | solution.py:35
  188.4 68.6 %copy-start.1 = (f32[16,8,16,128]{3,2,1,0:T(8,128)S(1)}, f32[16,8,16,128]{3,2,1,0:T(8,128)}, u32[]{:S(2)}) copy-start(f32[16,8,16,128]{3,2,1,0:T(8,128)} %param.42) | copy-start | bytes 3145732
  188.4 68.6 %all-gather.11.cloned.1.call-start = ((), (), s32[]{:S(2)}) async-start(), calls=%async_computation.10 | async-start | bytes 1572864 | tf_op jit(solution)/shard_map/all_gather | solution.py:127
  (1 other events, 12.3 us)
Sparse Core Ops, SparseCore 0:
  33.7 46.5 all-gather.4
  83.9 19.5 all-gather.6
  142.9 20.2 reduce-scatter.1
  188.6 45.3 all-gather.8
  237.5 19.4 all-gather.10
where the time goes:
time: 267 us; the launch traced here: 266 us
  waiting for transfers between devices  154 us (58%)
  blocking collectives  47.6 us (18%)
  local copies, waits for them, and re-layouts  15.1 us (6%)
  starting transfers between devices  14.7 us (6%)
  between operations  13.6 us (5%)
  other arithmetic  11.9 us (4%)
  matrix products  9.28 us (3%)
    all_gather x2, waiting for transfers between devices, spread_field(): portion = lax.all_gather(halfway, 'lon', axis=2, tiled=True)  92 us
    all_to_all x2, blocking collectives, spread_field(): lax.all_to_all(stacked, 'lat', split_axis=0, concat_axis=1, tiled=True)  25.1 us
    all_to_all x2, blocking collectives, spread_field(): lax.all_to_all(across, 'lat', split_axis=1, concat_axis=0, tiled=True)  22.4 us
    reduce_scatter x1, waiting for transfers between devices, per_device(): lax.psum_scatter(weights_here * coarse_grad[None], 'tm', scatter_dimensio...  20.4 us
    all_gather x1, waiting for transfers between devices, per_device(): return control + lax.all_gather(adjoint_mine, 'tm', axis=0, tiled=True)  19.6 us
    all_gather x1, waiting for transfers between devices, per_device(): lax.all_gather(spread_mine, 'tm', axis=0, tiled=True) * weights_here  9.88 us
    ppermute x4, starting transfers between devices, extended(): after = lax.ppermute(first, axis, down)  8.39 us
    ppermute x4, waiting for transfers between devices, extended(): before = lax.ppermute(last, axis, up)  7.34 us
  transfers between devices with their start and end apart: 14, of which 12 were waited for; matrix products, arithmetic and copies ran while one was open for 2% of the time, Pallas kernels for 0%

commit v1 on v0

v1 whole, which is shorter than its diff:
```python
import functools

import jax
import jax.numpy as jnp
from jax import lax
from jax.experimental import pallas as pl
from jax.experimental.pallas import tpu as pltpu
from jax.sharding import PartitionSpec as P

HIGHEST = lax.Precision.HIGHEST
F32 = jnp.float32
BF16 = jnp.bfloat16


def swap(x, axis, k):
    n = lax.axis_size(axis)
    return lax.ppermute(x, axis, [(i, i ^ k) for i in range(n)])


def two_pass(x, w, dims):
    high = x.astype(BF16)
    low = (x - high.astype(F32)).astype(BF16)
    dot = functools.partial(
        lax.dot_general, dimension_numbers=dims, preferred_element_type=F32
    )
    return dot(high, w) + dot(low, w)


def vmem_call(kernel, out_shape, flops, nbytes, scratch=(), smem=0, total=0):
    specs = [pl.BlockSpec(memory_space=pltpu.SMEM)] * smem
    specs += [pl.BlockSpec(memory_space=pltpu.VMEM)] * (total - smem)
    return pl.pallas_call(
        kernel,
        out_shape=out_shape,
        in_specs=specs,
        out_specs=jax.tree.map(lambda _: pl.BlockSpec(memory_space=pltpu.VMEM), out_shape),
        scratch_shapes=list(scratch),
        cost_estimate=pl.CostEstimate(flops=flops, bytes_accessed=nbytes, transcendentals=0),
    )


def increment_kernel(bands, slots, *refs):
    fields = refs[:bands]
    table = refs[bands]
    pert = refs[bands + 1 : bands + 1 + slots * bands]
    outs = refs[bands + 1 + slots * bands :]
    width = fields[0].shape[1]
    rows = outs[0].shape[0]
    shares = fields[0].shape[0] // rows
    source = jnp.concatenate([f[...] for f in fields], axis=1)
    spread = two_pass(source, table[...], (((1,), (1,)), ((), ())))
    for q in range(slots):
        for k in range(bands):
            total = None
            for m in range(shares):
                part = spread[m * rows : (m + 1) * rows, k * width : (k + 1) * width]
                part = part * pert[q * bands + k][m * rows : (m + 1) * rows, :].astype(F32)
                total = part if total is None else total + part
            outs[q][:, k * width : (k + 1) * width] = total


def adjoint_kernel(bands, slots, *refs):
    grads = refs[:slots]
    table = refs[slots]
    pert = refs[slots + 1 : slots + 1 + slots * bands]
    outs = refs[slots + 1 + slots * bands :]
    width = outs[0].shape[1]
    rows = grads[0].shape[0]
    shares = outs[0].shape[0] // rows
    columns = []
    for k in range(bands):
        pieces = []
        for m in range(shares):
            total = None
            for q in range(slots):
                part = grads[q][:, k * width : (k + 1) * width]
                part = part * pert[q * bands + k][m * rows : (m + 1) * rows, :].astype(F32)
                total = part if total is None else total + part
            pieces.append(total)
        columns.append(jnp.concatenate(pieces, axis=0))
    source = jnp.concatenate(columns, axis=1)
    result = two_pass(source, table[...], (((1,), (0,)), ((), ())))
    for k in range(bands):
        outs[k][...] = result[:, k * width : (k + 1) * width]


def observe_kernel(bands, levels, rows, padded, width, *refs):
    places = refs[0]
    inc, low, high = refs[1:4]
    lists = refs[4 : 4 + bands]
    out, window, grad = refs[4 + bands :]
    filler = jnp.zeros((padded - rows - 2, width), F32)
    for k in range(bands):
        span = slice(k * width, (k + 1) * width)
        for level in range(levels):
            block = [
                inc[level * rows : (level + 1) * rows, span],
                low[level : level + 1, span],
                high[level : level + 1, span],
                filler,
            ]
            window[k, level * padded : (level + 1) * padded, :] = jnp.concatenate(block, axis=0)
    grad[...] = jnp.zeros_like(grad)
    lane = lax.broadcasted_iota(jnp.int32, (levels * padded, width), 1)
    first = places[2 * bands].astype(F32)
    for k in range(bands):
        before, after = places[k], places[bands + k]
        main = lists[k][:width, :]
        rowpart = lists[k][width : width + padded, :]
        tail = width + padded
        left = lists[k][tail : tail + 1, :]
        right = lists[k][tail + 1 : tail + 2, :]
        level_of = lists[k][tail + 2 : tail + 3, :]
        value = lists[k][tail + 3 : tail + 4, :]
        weight = lists[k][tail + 4 : tail + 5, :]
        seen_by = lax.dot_general(
            window[k], main, (((1,), (0,)), ((), ())),
            precision=HIGHEST, preferred_element_type=F32,
        )
        seen_by += window[before][:, width - 1 : width] * left
        seen_by += window[after][:, 0:1] * right
        chosen = jnp.concatenate(
            [jnp.where(level_of == first + level, rowpart, 0.0) for level in range(levels)], axis=0
        )
        seen = jnp.sum(chosen * seen_by, axis=0, keepdims=True)
        weighted = chosen * (weight * (seen - value))
        grad[k] += lax.dot_general(
            weighted, main, (((1,), (1,)), ((), ())),
            precision=HIGHEST, preferred_element_type=F32,
        )
        onto_left = jnp.sum(weighted * left, axis=1, keepdims=True)
        onto_right = jnp.sum(weighted * right, axis=1, keepdims=True)
        grad[before] += jnp.where(lane == width - 1, onto_left, 0.0)
        grad[after] += jnp.where(lane == 0, onto_right, 0.0)
    for k in range(bands):
        out[:, k * width : (k + 1) * width] = grad[k]


def per_device(
    control,
    ens_pert,
    lat_filter,
    lon_filter,
    interp_lat,
    interp_lon,
    obs_cell,
    obs_count,
    obs_value,
    obs_weight,
):
    slots, lats, lons = (lax.axis_size(axis) for axis in ("tm", "lat", "lon"))
    t, a, b = (lax.axis_index(axis) for axis in ("tm", "lat", "lon"))
    members, levels, rows, width = control.shape
    share = members // slots
    group = levels // lons
    fields = share * group * rows
    fine_rows, fine_cols = interp_lat.shape[0], interp_lon.shape[0]
    padded = -(-(rows + 2) // 8) * 8
    slot_pert = ens_pert[0]

    slot_range = jnp.arange(obs_cell.shape[-1])
    usable = (slot_range < obs_count[0, :, 0, 0, None]).astype(F32)
    held = jnp.stack(
        [
            obs_cell[0, :, 0, 0].astype(F32),
            obs_value[0, :, 0, 0],
            obs_weight[0, :, 0, 0] * usable,
        ],
        axis=1,
    )
    own_lists = [lax.dynamic_index_in_dim(held, t, 0, False)]
    for q in range(1, slots):
        own_lists.append(swap(lax.dynamic_index_in_dim(held, t ^ q, 0, False), "tm", q))
    package = jnp.concatenate(own_lists, axis=1)
    cells = package[0].astype(jnp.int32)
    level_of = cells // (fine_rows * fine_cols)
    row_of = (cells // fine_cols) % fine_rows
    col_of = cells % fine_cols
    row_hot = (jnp.arange(fine_rows)[:, None] == row_of[None, :]).astype(F32)
    col_hot = (jnp.arange(fine_cols)[:, None] == col_of[None, :]).astype(F32)
    row_part = jnp.einsum("ip,io->po", interp_lat, row_hot, precision=HIGHEST)
    col_part = jnp.einsum("jq,jo->qo", interp_lon, col_hot, precision=HIGHEST)
    blank = functools.partial(jnp.zeros, dtype=F32)
    count = cells.shape[0]
    listing = jnp.concatenate(
        [
            col_part[1 : width + 1],
            row_part[1 : rows + 1],
            row_part[:1],
            row_part[rows + 1 :],
            blank((padded - rows - 2, count)),
            col_part[:1],
            col_part[width + 1 :],
            level_of.astype(F32)[None],
            package[1:3],
            blank((3, count)),
        ],
        axis=0,
    )

    def level_slice(x, k):
        return lax.dynamic_slice_in_dim(x, (b ^ k) * group, group, 1)

    def member_slice(x, q):
        return lax.dynamic_slice_in_dim(x, (t ^ q) * share, share, 0)

    def to_group(x):
        pieces = [level_slice(x, 0).astype(F32)]
        for k in range(1, lons):
            pieces.append(swap(level_slice(x, k).astype(F32), "lon", k))
        return [p.reshape(fields, width) for p in pieces]

    crossing = [swap(member_slice(slot_pert, q).astype(F32), "tm", q) for q in range(1, slots)]
    pert = to_group(member_slice(slot_pert, 0))
    for x in crossing:
        pert += to_group(x)

    lat_matrix = lat_filter.astype(F32)

    def lat_block(i, j):
        return lax.dynamic_slice(lat_matrix, (i * rows, j * rows), (rows, rows))

    def lat_mix(x, block):
        other = swap(x, "lat", 1)
        total = None
        for h in range(0, lats, 2):
            part = jnp.einsum("ab,mbk->mak", block(a ^ h, a), x, precision=HIGHEST)
            part += jnp.einsum("ab,mbk->mak", block(a ^ h, a ^ 1), other, precision=HIGHEST)
            total = part if h == 0 else total + swap(part, "lat", h)
        return total

    mine = member_slice(control, 0).reshape(share * levels, rows, width)
    mixed = lat_mix(mine, lat_block).reshape(share, levels, rows, width)
    source = to_group(mixed)

    listings = [listing] + [swap(listing, "lon", k) for k in range(1, lons)]

    tall = jnp.concatenate(
        [lax.dynamic_slice_in_dim(lon_filter, (b ^ k) * width, width, 0) for k in range(lons)], axis=0
    )
    table = jnp.concatenate(
        [lax.dynamic_slice_in_dim(tall, (b ^ k) * width, width, 1) for k in range(lons)], axis=1
    )
    whole = lons * width
    lines = group * rows
    flops = 4 * fields * whole * whole
    nbytes = 4 * fields * whole * (1 + slots) + 2 * whole * whole + 4 * slots * lines * whole
    partial = vmem_call(
        functools.partial(increment_kernel, lons, slots),
        [jax.ShapeDtypeStruct((lines, whole), F32)] * slots,
        flops,
        nbytes,
        total=lons + 1 + slots * lons,
    )(*source, table, *pert)
    increment = partial[0]
    for q in range(1, slots):
        increment = increment + swap(partial[q], "tm", q)

    up = [(i, i + 1) for i in range(lats - 1)]
    down = [(i + 1, i) for i in range(lats - 1)]
    by_level = increment.reshape(group, rows, whole)
    low = lax.ppermute(by_level[:, rows - 1], "lat", up)
    high = lax.ppermute(by_level[:, 0], "lat", down)
    order = jnp.arange(lons)
    band = b ^ order
    places = jnp.concatenate([b ^ ((band - 1) % lons), b ^ ((band + 1) % lons), (b * group)[None]])
    tall_rows = group * padded
    grad_pad = vmem_call(
        functools.partial(observe_kernel, lons, group, rows, padded, width),
        jax.ShapeDtypeStruct((tall_rows, whole), F32),
        24 * tall_rows * whole * count,
        4 * whole * (lines + tall_rows) + 4 * lons * listing.size,
        scratch=[pltpu.VMEM((lons, tall_rows, width), F32)] * 2,
        smem=1,
        total=4 + lons,
    )(places.astype(jnp.int32), increment, low, high, *listings)
    grad_pad = grad_pad.reshape(group, padded, whole)
    to_last = lax.ppermute(grad_pad[:, rows], "lat", down)
    to_first = lax.ppermute(grad_pad[:, rows + 1], "lat", up)
    coarse = jnp.concatenate(
        [
            grad_pad[:, :1] + to_first[:, None],
            grad_pad[:, 1 : rows - 1],
            grad_pad[:, rows - 1 : rows] + to_last[:, None],
        ],
        axis=1,
    ).reshape(lines, whole)
    coarses = [coarse] + [swap(coarse, "tm", q) for q in range(1, slots)]

    pieces = vmem_call(
        functools.partial(adjoint_kernel, lons, slots),
        [jax.ShapeDtypeStruct((fields, width), F32)] * lons,
        flops,
        nbytes,
        total=slots + 1 + slots * lons,
    )(*coarses, table, *pert)
    shape = (share, group, rows, width)
    pieces = [pieces[0]] + [swap(pieces[k], "lon", k) for k in range(1, lons)]

    def lat_block_t(i, j):
        return lat_block(j, i).T

    result = control
    step = max(lons // 2, 1)
    for start in range(0, lons, step):
        some = jnp.stack(pieces[start : start + step]).reshape(step * share * group, rows, width)
        some = lat_mix(some, lat_block_t)
        for q in range(slots):
            arrived = some if q == 0 else swap(some, "tm", q)
            arrived = arrived.reshape((step,) + shape)
            for k in range(step):
                at = ((t ^ q) * share, (b ^ (start + k)) * group, 0, 0)
                old = lax.dynamic_slice(control, at, shape)
                result = lax.dynamic_update_slice(result, old + arrived[k], at)
    return result


def solution(mesh):
    placed = (
        P(None, None, "lat", "lon"),
        P("tm", None, None, "lat", "lon"),
        P(),
        P(),
        P("lat", None),
        P("lon", None),
        P("tm", None, "lat", "lon", None),
        P("tm", None, "lat", "lon"),
        P("tm", None, "lat", "lon", None),
        P("tm", None, "lat", "lon", None),
    )
    return jax.shard_map(
        per_device,
        mesh=mesh,
        in_specs=placed,
        out_specs=P(None, None, "lat", "lon"),
        check_vma=False,
    )
```

time: 267 us -> 147 us (0.55)
  waiting for transfers between devices: 154 us -> 68 us
  blocking collectives: 47.6 us -> 0 us
  starting transfers between devices: 14.7 us -> 43.3 us
  between operations: 13.6 us -> 0.69 us
  Pallas kernels: 0 us -> 8.22 us
  other arithmetic: 11.9 us -> 6.09 us
    all_gather x4 -> x0, waiting for transfers between devices: 122 us -> none  [the longest x2 92 us: spread_field(): portion = lax.all_gather(halfway, 'lon', axis=2, tiled=True)]
    ppermute x8 -> x31, waiting for transfers between devices: 9.52 us -> 68 us  [the longest x27 63.6 us: swap(): return lax.ppermute(x, axis, [(i, i ^ k) for i in range(n)])]
    all_to_all x4 -> x0, blocking collectives: 47.6 us -> none  [the longest x2 25.1 us: spread_field(): lax.all_to_all(stacked, 'lat', split_axis=0, concat_axis=1, tiled=True)]
    ppermute x8 -> x31, starting transfers between devices: 11.3 us -> 43.3 us  [the longest x27 35.1 us: swap(): return lax.ppermute(x, axis, [(i, i ^ k) for i in range(n)])]
    reduce_scatter x1 -> x0, waiting for transfers between devices: 20.4 us -> none  [per_device(): lax.psum_scatter(weights_here * coarse_grad[None], 'tm', scatter_dimensio...]
    pallas_call x0 -> x3, Pallas kernels: none -> 8.22 us  [the longest x1 2.77 us: per_device(): vmem_call(functools.partial(observe_kernel, lons, group, rows, padded, wi...]
    unnamed x34 -> x84, local copies, waits for them, and re-layouts: 1.63 us -> 7.21 us
    another operation x5 -> x3, other arithmetic: 3.53 us -> 0.04 us  [the longest x2 0.04 us: per_device(): jnp.stack(pieces[start:start + step])]
  transfers between devices with their start and end apart: 14 -> 31, of which waited for: 12 -> 13; matrix products, arithmetic and copies ran while one was open for 2% -> 11% of each run, Pallas kernels for 0% -> 0%
where the time goes in v1:
time: 147 us; the launch traced here: 146 us
  waiting for transfers between devices  68 us (46%)
  starting transfers between devices  43.3 us (29%)
  local copies, waits for them, and re-layouts  12.5 us (9%)
  Pallas kernels  8.22 us (6%)
  matrix products  7.32 us (5%)
  other arithmetic  6.09 us (4%)
    ppermute x27, waiting for transfers between devices, swap(): return lax.ppermute(x, axis, [(i, i ^ k) for i in range(n)])  63.6 us
    ppermute x27, starting transfers between devices, swap(): return lax.ppermute(x, axis, [(i, i ^ k) for i in range(n)])  35.1 us
    unnamed x84, local copies, waits for them, and re-layouts  7.21 us
    ppermute x1, starting transfers between devices, per_device(): to_first = lax.ppermute(grad_pad[:, rows + 1], 'lat', up)  4.27 us
    dot_general x6, matrix products, lat_mix(): part = jnp.einsum('ab,mbk->mak', block(a ^ h, a), x, precision=HIGHEST)  3.85 us
    ppermute x1, waiting for transfers between devices, per_device(): to_last = lax.ppermute(grad_pad[:, rows], 'lat', down)  3.63 us
    dot_general x6, matrix products, lat_mix(): jnp.einsum('ab,mbk->mak', block(a ^ h, a ^ 1), other, precision=HIGHEST)  3.12 us
  transfers between devices with their start and end apart: 31, of which 13 were waited for; matrix products, arithmetic and copies ran while one was open for 11% of the time, Pallas kernels for 0%

profile of v1, /device:TPU:0, one launch (start us, length us, event | category | flops | bytes accessed | tf_op | source)
XLA Modules:
  0.0 146.1 jit_solution(2148097916567963171)
XLA Ops:
  1.8 2.6 %collective-permute-start.8 = (f32[8,8,16,128]{3,2,1,0:T(8,128)S(1)}, f32[8,8,16,128]{3,2,1,0:T(8,128)S(1)}, u32[]{:S(2)}, u32[]{:S(2)}) collective-permute-start(f32[8,8,16,128]{3,2,1,0:T(8,128)S(1)} %bitcast_convert_fusion), channel_id=1, source_target_pairs={{0,16},{16,0},{1,17},{17,1},{2,18},{18,2},{3,19},{19,3},{4,20},{20... | collective-permute-start | bytes 1572872 | tf_op jit(solution)/shard_map/ppermute | solution.py:17
  6.7 2.6 %collective-permute-start.6 = (f32[8,2,16,128]{3,2,1,0:T(8,128)}, f32[8,2,16,128]{3,2,1,0:T(8,128)S(1)}, u32[]{:S(2)}, u32[]{:S(2)}) collective-permute-start(f32[8,2,16,128]{3,2,1,0:T(8,128)} %get-tuple-element.24), channel_id=1, source_target_pairs={{0,2},{1,3},{2,0},{3,1},{4,6},{5,7},{6,4},{7,5},{8,10},{9,11},{10,... | collective-permute-start | bytes 393224 | tf_op jit(solution)/shard_map/ppermute | solution.py:17
  18.2 2.8 %collective-permute-start.7 = (f32[8,2,16,128]{3,2,1,0:T(8,128)}, f32[8,2,16,128]{3,2,1,0:T(8,128)}, u32[]{:S(2)}, u32[]{:S(2)}) collective-permute-start(f32[8,2,16,128]{3,2,1,0:T(8,128)} %get-tuple-element.23), channel_id=1, source_target_pairs={{0,3},{1,2},{2,1},{3,0},{4,7},{5,6},{6,5},{7,4},{8,11},{9,10},{10,... | collective-permute-start | bytes 393224 | tf_op jit(solution)/shard_map/ppermute | solution.py:17
  22.8 1.6 %collective-permute-start.1 = (f32[64,16,128]{2,1,0:T(8,128)S(1)}, f32[64,16,128]{2,1,0:T(8,128)S(1)}, u32[]{:S(2)}, u32[]{:S(2)}) collective-permute-start(f32[64,16,128]{2,1,0:T(8,128)S(1)} %fusion), channel_id=1, source_target_pairs={{0,8},{4,12},{8,0},{12,4},{1,9},{5,13},{9,1},{13,5},{2,10},{6,14},... | collective-permute-start | bytes 1572872 | tf_op jit(solution)/shard_map/ppermute | solution.py:17
  25.4 10.6 %collective-permute-done.1 = f32[64,16,128]{2,1,0:T(8,128)S(1)} collective-permute-done((f32[64,16,128]{2,1,0:T(8,128)S(1)}, f32[64,16,128]{2,1,0:T(8,128)S(1)}, u32[]{:S(2)}, u32[]{:S(2)}) %collective-permute-start.1) | collective-permute-done | bytes 524320 | tf_op jit(solution)/shard_map/ppermute | solution.py:17
  37.1 1.9 %collective-permute-start.11 = (f32[8,2,16,128]{3,2,1,0:T(8,128)S(1)}, f32[8,2,16,128]{3,2,1,0:T(8,128)S(1)}, u32[]{:S(2)}, u32[]{:S(2)}) collective-permute-start(f32[8,2,16,128]{3,2,1,0:T(8,128)S(1)} %get-tuple-element.19), channel_id=1, source_target_pairs={{0,3},{1,2},{2,1},{3,0},{4,7},{5,6},{6,5},{7,4},{8,11},{9,10},{10,... | collective-permute-start | bytes 393224 | tf_op jit(solution)/shard_map/ppermute | solution.py:17
  41.5 1.9 %collective-permute-start.4 = (f32[8,2,16,128]{3,2,1,0:T(8,128)S(1)}, f32[8,2,16,128]{3,2,1,0:T(8,128)S(1)}, u32[]{:S(2)}, u32[]{:S(2)}) collective-permute-start(f32[8,2,16,128]{3,2,1,0:T(8,128)S(1)} %get-tuple-element.35), channel_id=1, source_target_pairs={{0,3},{1,2},{2,1},{3,0},{4,7},{5,6},{6,5},{7,4},{8,11},{9,10},{10,... | collective-permute-start | bytes 393224 | tf_op jit(solution)/shard_map/ppermute | solution.py:17
  43.6 8.6 %collective-permute-done.10 = f32[8,2,16,128]{3,2,1,0:T(8,128)S(1)} collective-permute-done((f32[8,2,16,128]{3,2,1,0:T(8,128)S(1)}, f32[8,2,16,128]{3,2,1,0:T(8,128)S(1)}, u32[]{:S(2)}, u32[]{:S(2)}) %collective-permute-start.10) | collective-permute-done | bytes 131104 | tf_op jit(solution)/shard_map/ppermute | solution.py:17
  52.1 5.6 %collective-permute-done.3 = f32[8,2,16,128]{3,2,1,0:T(8,128)S(1)} collective-permute-done((f32[8,2,16,128]{3,2,1,0:T(8,128)S(1)}, f32[8,2,16,128]{3,2,1,0:T(8,128)S(1)}, u32[]{:S(2)}, u32[]{:S(2)}) %collective-permute-start.3) | collective-permute-done | bytes 131104 | tf_op jit(solution)/shard_map/ppermute | solution.py:17
  58.4 2.7 %shard_map.100 = (f32[32,512]{1,0:T(8,128)}, f32[32,512]{1,0:T(8,128)}) custom-call(f32[256,128]{1,0:T(8,128)} %bitcast.179, f32[256,128]{1,0:T(8,128)} %bitcast.186, f32[256,128]{1,0:T(8,128)} %bitcast.187, f32[256,128]{1,0:T(8,128)} %bitcast.188, bf16[512,512]{1,0:T(8,128)(2,1)} %pad_maximum_fusion.1.refs_4_.refs_2_, ...), custom_call_target="tpu_custom_call" | custom-call | flops 268435456 | bytes 2228224 | tf_op jit(solution)/shard_map/pallas_call | solution.py:248
  62.8 2.1 %collective-permute-start.16 = (f32[160,128]{1,0:T(8,128)S(1)}, f32[160,128]{1,0:T(8,128)S(1)}, u32[]{:S(2)}, u32[]{:S(2)}) collective-permute-start(f32[160,128]{1,0:T(8,128)S(1)} %concatenate.22.refs_4_), channel_id=1, source_target_pairs={{0,1},{1,0},{2,3},{3,2},{4,5},{5,4},{6,7},{7,6},{8,9},{9,8},{10,11... | collective-permute-start | bytes 245768 | tf_op jit(solution)/shard_map/ppermute | solution.py:17
  65.3 2.1 %collective-permute-start.18 = (f32[160,128]{1,0:T(8,128)S(1)}, f32[160,128]{1,0:T(8,128)S(1)}, u32[]{:S(2)}, u32[]{:S(2)}) collective-permute-start(f32[160,128]{1,0:T(8,128)S(1)} %concatenate.22.refs_4_), channel_id=1, source_target_pairs={{0,3},{1,2},{2,1},{3,0},{4,7},{5,6},{6,5},{7,4},{8,11},{9,10},{10,... | collective-permute-start | bytes 245768 | tf_op jit(solution)/shard_map/ppermute | solution.py:17
  74.1 2.8 %shard_map.101 = f32[48,512]{1,0:T(8,128)} custom-call(s32[9]{0:T(128)} %pad_add_fusion.refs_0_, f32[32,512]{1,0:T(8,128)} %copy-done.16, f32[2,512]{1,0:T(2,128)} %copy-done.30, f32[2,512]{1,0:T(2,128)} %copy-done.31, f32[160,128]{1,0:T(8,128)} %copy-done.15, f32[160,128]{1,0:T(8,128)} %copy-done.24, f32[160,128]{1,0:T(8,128)} %copy-done.25, ...), custom_call_target="tpu_custom_call" | custom-call | flops 75497472 | bytes 491520 | tf_op jit(solution)/shard_map/pallas_call | solution.py:268
  79.0 3.6 %collective-permute-done.20 = f32[2,512]{1,0:T(2,128)S(1)} collective-permute-done((f32[2,512]{1,0:T(2,128)S(1)}, f32[2,512]{1,0:T(2,128)S(1)}, u32[]{:S(2)}, u32[]{:S(2)}) %collective-permute-start.20) | collective-permute-done | bytes 4128 | tf_op jit(solution)/shard_map/ppermute | solution.py:278
  83.4 4.3 %collective-permute-start.19 = (f32[2,512]{1,0:T(2,128)S(1)}, f32[2,512]{1,0:T(2,128)S(1)}, u32[]{:S(2)}, u32[]{:S(2)}) collective-permute-start(f32[2,512]{1,0:T(2,128)S(1)} %bitcast.196), channel_id=1, source_target_pairs={{0,4},{4,8},{8,12},{1,5},{5,9},{9,13},{2,6},{6,10},{10,14},{3,7},{... | collective-permute-start | bytes 12296 | tf_op jit(solution)/shard_map/ppermute | solution.py:279
  89.3 3.7 %collective-permute-done.21.refs_1_ = f32[32,512]{1,0:T(8,128)S(1)} collective-permute-done((f32[32,512]{1,0:T(8,128)S(1)}, f32[32,512]{1,0:T(8,128)S(1)}, u32[]{:S(2)}, u32[]{:S(2)}) %collective-permute-start.21) | collective-permute-done | bytes 65568 | tf_op jit(solution)/shard_map/ppermute | solution.py:17
  93.6 2.7 %shard_map.102 = (f32[256,128]{1,0:T(8,128)}, f32[256,128]{1,0:T(8,128)}, f32[256,128]{1,0:T(8,128)}, f32[256,128]{1,0:T(8,128)}) custom-call(f32[32,512]{1,0:T(8,128)} %bitcast.185, f32[32,512]{1,0:T(8,128)} %copy-done.28, bf16[512,512]{1,0:T(8,128)(2,1)} %pad_maximum_fusion.1.refs_4_.refs_2_, f32[256,128]{1,0:T(8,128)} %bitcast_convert_fusion.4.refs_5_.refs_3_, ...), custom_call_target="tpu_custom_call" | custom-call | flops 268435456 | bytes 2228224 | tf_op jit(solution)/shard_map/pallas_call | solution.py:290
  97.7 2.1 %collective-permute-start.27 = (f32[256,128]{1,0:T(8,128)}, f32[256,128]{1,0:T(8,128)S(1)}, u32[]{:S(2)}, u32[]{:S(2)}) collective-permute-start(f32[256,128]{1,0:T(8,128)} %get-tuple-element.16), channel_id=1, source_target_pairs={{0,3},{1,2},{2,1},{3,0},{4,7},{5,6},{6,5},{7,4},{8,11},{9,10},{10,... | collective-permute-start | bytes 393224 | tf_op jit(solution)/shard_map/ppermute | solution.py:17
  99.8 8.4 %collective-permute-done.26 = f32[256,128]{1,0:T(8,128)S(1)} collective-permute-done((f32[256,128]{1,0:T(8,128)}, f32[256,128]{1,0:T(8,128)S(1)}, u32[]{:S(2)}, u32[]{:S(2)}) %collective-permute-start.26) | collective-permute-done | bytes 131104 | tf_op jit(solution)/shard_map/ppermute | solution.py:17
  109.0 2.8 %collective-permute-start.22 = (f32[256,128]{1,0:T(8,128)S(1)}, f32[256,128]{1,0:T(8,128)S(1)}, u32[]{:S(2)}, u32[]{:S(2)}) collective-permute-start(f32[256,128]{1,0:T(8,128)S(1)} %copy-done.38), channel_id=1, source_target_pairs={{0,1},{1,0},{2,3},{3,2},{4,5},{5,4},{6,7},{7,6},{8,9},{9,8},{10,11... | collective-permute-start | bytes 393224 | tf_op jit(solution)/shard_map/ppermute | solution.py:17
  111.8 3.4 %collective-permute-done.22 = f32[256,128]{1,0:T(8,128)S(1)} collective-permute-done((f32[256,128]{1,0:T(8,128)S(1)}, f32[256,128]{1,0:T(8,128)S(1)}, u32[]{:S(2)}, u32[]{:S(2)}) %collective-permute-start.22) | collective-permute-done | bytes 131104 | tf_op jit(solution)/shard_map/ppermute | solution.py:17
  119.9 10.6 %collective-permute-done.24 = f32[32,16,128]{2,1,0:T(8,128)S(1)} collective-permute-done((f32[32,16,128]{2,1,0:T(8,128)S(1)}, f32[32,16,128]{2,1,0:T(8,128)S(1)}, u32[]{:S(2)}, u32[]{:S(2)}) %collective-permute-start.24) | collective-permute-done | bytes 262176 | tf_op jit(solution)/shard_map/ppermute | solution.py:17
  133.6 6.5 %collective-permute-done.25 = f32[32,16,128]{2,1,0:T(8,128)S(1)} collective-permute-done((f32[32,16,128]{2,1,0:T(8,128)S(1)}, f32[32,16,128]{2,1,0:T(8,128)S(1)}, u32[]{:S(2)}, u32[]{:S(2)}) %collective-permute-start.25) | collective-permute-done | bytes 262176 | tf_op jit(solution)/shard_map/ppermute | solution.py:17
  140.3 4.1 %collective-permute-done.30 = f32[32,16,128]{2,1,0:T(8,128)S(1)} collective-permute-done((f32[32,16,128]{2,1,0:T(8,128)S(1)}, f32[32,16,128]{2,1,0:T(8,128)S(1)}, u32[]{:S(2)}, u32[]{:S(2)}) %collective-permute-start.30) | collective-permute-done | bytes 262176 | tf_op jit(solution)/shard_map/ppermute | solution.py:17
  (187 shorter events, 45.5 us)
Async XLA Ops:
  1.2 20.5 %collective-permute-start = (f32[64,16,128]{2,1,0:T(8,128)S(1)}, f32[64,16,128]{2,1,0:T(8,128)S(1)}, u32[]{:S(2)}, u32[]{:S(2)}) collective-permute-start(f32[64,16,128]{2,1,0:T(8,128)S(1)} %bitcast.149), channel_id=1, source_target_pairs={{0,4},{4,0},{8,12},{12,8},{1,5},{5,1},{9,13},{13,9},{2,6},{6,2},{1... | collective-permute-start | bytes 1572872 | tf_op jit(solution)/shard_map/ppermute | solution.py:17
  1.8 22.9 %collective-permute-start.8 = (f32[8,8,16,128]{3,2,1,0:T(8,128)S(1)}, f32[8,8,16,128]{3,2,1,0:T(8,128)S(1)}, u32[]{:S(2)}, u32[]{:S(2)}) collective-permute-start(f32[8,8,16,128]{3,2,1,0:T(8,128)S(1)} %bitcast_convert_fusion), channel_id=1, source_target_pairs={{0,16},{16,0},{1,17},{17,1},{2,18},{18,2},{3,19},{19,3},{4,20},{20... | collective-permute-start | bytes 1572872 | tf_op jit(solution)/shard_map/ppermute | solution.py:17
  5.1 32.0 %collective-permute-start.5 = (f32[8,2,16,128]{3,2,1,0:T(8,128)}, f32[8,2,16,128]{3,2,1,0:T(8,128)S(1)}, u32[]{:S(2)}, u32[]{:S(2)}) collective-permute-start(f32[8,2,16,128]{3,2,1,0:T(8,128)} %get-tuple-element.25), channel_id=1, source_target_pairs={{0,1},{1,0},{2,3},{3,2},{4,5},{5,4},{6,7},{7,6},{8,9},{9,8},{10,11... | collective-permute-start | bytes 393224 | tf_op jit(solution)/shard_map/ppermute | solution.py:17
  6.7 32.3 %collective-permute-start.6 = (f32[8,2,16,128]{3,2,1,0:T(8,128)}, f32[8,2,16,128]{3,2,1,0:T(8,128)S(1)}, u32[]{:S(2)}, u32[]{:S(2)}) collective-permute-start(f32[8,2,16,128]{3,2,1,0:T(8,128)} %get-tuple-element.24), channel_id=1, source_target_pairs={{0,2},{1,3},{2,0},{3,1},{4,6},{5,7},{6,4},{7,5},{8,10},{9,11},{10,... | collective-permute-start | bytes 393224 | tf_op jit(solution)/shard_map/ppermute | solution.py:17
  18.2 22.5 %collective-permute-start.7 = (f32[8,2,16,128]{3,2,1,0:T(8,128)}, f32[8,2,16,128]{3,2,1,0:T(8,128)}, u32[]{:S(2)}, u32[]{:S(2)}) collective-permute-start(f32[8,2,16,128]{3,2,1,0:T(8,128)} %get-tuple-element.23), channel_id=1, source_target_pairs={{0,3},{1,2},{2,1},{3,0},{4,7},{5,6},{6,5},{7,4},{8,11},{9,10},{10,... | collective-permute-start | bytes 393224 | tf_op jit(solution)/shard_map/ppermute | solution.py:17
  22.8 13.1 %collective-permute-start.1 = (f32[64,16,128]{2,1,0:T(8,128)S(1)}, f32[64,16,128]{2,1,0:T(8,128)S(1)}, u32[]{:S(2)}, u32[]{:S(2)}) collective-permute-start(f32[64,16,128]{2,1,0:T(8,128)S(1)} %fusion), channel_id=1, source_target_pairs={{0,8},{4,12},{8,0},{12,4},{1,9},{5,13},{9,1},{13,5},{2,10},{6,14},... | collective-permute-start | bytes 1572872 | tf_op jit(solution)/shard_map/ppermute | solution.py:17
  25.4 16.2 %collective-permute-start.9 = (f32[8,2,16,128]{3,2,1,0:T(8,128)S(1)}, f32[8,2,16,128]{3,2,1,0:T(8,128)S(1)}, u32[]{:S(2)}, u32[]{:S(2)}) collective-permute-start(f32[8,2,16,128]{3,2,1,0:T(8,128)S(1)} %get-tuple-element.21), channel_id=1, source_target_pairs={{0,1},{1,0},{2,3},{3,2},{4,5},{5,4},{6,7},{7,6},{8,9},{9,8},{10,11... | collective-permute-start | bytes 393224 | tf_op jit(solution)/shard_map/ppermute | solution.py:17
  35.9 16.2 %collective-permute-start.10 = (f32[8,2,16,128]{3,2,1,0:T(8,128)S(1)}, f32[8,2,16,128]{3,2,1,0:T(8,128)S(1)}, u32[]{:S(2)}, u32[]{:S(2)}) collective-permute-start(f32[8,2,16,128]{3,2,1,0:T(8,128)S(1)} %get-tuple-element.20), channel_id=1, source_target_pairs={{0,2},{1,3},{2,0},{3,1},{4,6},{5,7},{6,4},{7,5},{8,10},{9,11},{10,... | collective-permute-start | bytes 393224 | tf_op jit(solution)/shard_map/ppermute | solution.py:17
  37.1 15.0 %collective-permute-start.11 = (f32[8,2,16,128]{3,2,1,0:T(8,128)S(1)}, f32[8,2,16,128]{3,2,1,0:T(8,128)S(1)}, u32[]{:S(2)}, u32[]{:S(2)}) collective-permute-start(f32[8,2,16,128]{3,2,1,0:T(8,128)S(1)} %get-tuple-element.19), channel_id=1, source_target_pairs={{0,3},{1,2},{2,1},{3,0},{4,7},{5,6},{6,5},{7,4},{8,11},{9,10},{10,... | collective-permute-start | bytes 393224 | tf_op jit(solution)/shard_map/ppermute | solution.py:17
  39.0 13.1 %collective-permute-start.2 = (f32[8,2,16,128]{3,2,1,0:T(8,128)S(1)}, f32[8,2,16,128]{3,2,1,0:T(8,128)S(1)}, u32[]{:S(2)}, u32[]{:S(2)}) collective-permute-start(f32[8,2,16,128]{3,2,1,0:T(8,128)S(1)} %get-tuple-element.37), channel_id=1, source_target_pairs={{0,1},{1,0},{2,3},{3,2},{4,5},{5,4},{6,7},{7,6},{8,9},{9,8},{10,11... | collective-permute-start | bytes 393224 | tf_op jit(solution)/shard_map/ppermute | solution.py:17
  40.6 17.1 %collective-permute-start.3 = (f32[8,2,16,128]{3,2,1,0:T(8,128)S(1)}, f32[8,2,16,128]{3,2,1,0:T(8,128)S(1)}, u32[]{:S(2)}, u32[]{:S(2)}) collective-permute-start(f32[8,2,16,128]{3,2,1,0:T(8,128)S(1)} %get-tuple-element.36), channel_id=1, source_target_pairs={{0,2},{1,3},{2,0},{3,1},{4,6},{5,7},{6,4},{7,5},{8,10},{9,11},{10,... | collective-permute-start | bytes 393224 | tf_op jit(solution)/shard_map/ppermute | solution.py:17
  41.5 16.2 %collective-permute-start.4 = (f32[8,2,16,128]{3,2,1,0:T(8,128)S(1)}, f32[8,2,16,128]{3,2,1,0:T(8,128)S(1)}, u32[]{:S(2)}, u32[]{:S(2)}) collective-permute-start(f32[8,2,16,128]{3,2,1,0:T(8,128)S(1)} %get-tuple-element.35), channel_id=1, source_target_pairs={{0,3},{1,2},{2,1},{3,0},{4,7},{5,6},{6,5},{7,4},{8,11},{9,10},{10,... | collective-permute-start | bytes 393224 | tf_op jit(solution)/shard_map/ppermute | solution.py:17
  61.2 6.2 %collective-permute-start.12 = (f32[32,512]{1,0:T(8,128)}, f32[32,512]{1,0:T(8,128)S(1)}, u32[]{:S(2)}, u32[]{:S(2)}) collective-permute-start(f32[32,512]{1,0:T(8,128)} %get-tuple-element.12), channel_id=1, source_target_pairs={{0,16},{16,0},{1,17},{17,1},{2,18},{18,2},{3,19},{19,3},{4,20},{20... | collective-permute-start | bytes 196616 | tf_op jit(solution)/shard_map/ppermute | solution.py:17
  62.8 8.5 %collective-permute-start.16 = (f32[160,128]{1,0:T(8,128)S(1)}, f32[160,128]{1,0:T(8,128)S(1)}, u32[]{:S(2)}, u32[]{:S(2)}) collective-permute-start(f32[160,128]{1,0:T(8,128)S(1)} %concatenate.22.refs_4_), channel_id=1, source_target_pairs={{0,1},{1,0},{2,3},{3,2},{4,5},{5,4},{6,7},{7,6},{8,9},{9,8},{10,11... | collective-permute-start | bytes 245768 | tf_op jit(solution)/shard_map/ppermute | solution.py:17
  64.9 7.8 %collective-permute-start.17 = (f32[160,128]{1,0:T(8,128)S(1)}, f32[160,128]{1,0:T(8,128)S(1)}, u32[]{:S(2)}, u32[]{:S(2)}) collective-permute-start(f32[160,128]{1,0:T(8,128)S(1)} %concatenate.22.refs_4_), channel_id=1, source_target_pairs={{0,2},{1,3},{2,0},{3,1},{4,6},{5,7},{6,4},{7,5},{8,10},{9,11},{10,... | collective-permute-start | bytes 245768 | tf_op jit(solution)/shard_map/ppermute | solution.py:17
  65.3 7.5 %collective-permute-start.18 = (f32[160,128]{1,0:T(8,128)S(1)}, f32[160,128]{1,0:T(8,128)S(1)}, u32[]{:S(2)}, u32[]{:S(2)}) collective-permute-start(f32[160,128]{1,0:T(8,128)S(1)} %concatenate.22.refs_4_), channel_id=1, source_target_pairs={{0,3},{1,2},{2,1},{3,0},{4,7},{5,6},{6,5},{7,4},{8,11},{9,10},{10,... | collective-permute-start | bytes 245768 | tf_op jit(solution)/shard_map/ppermute | solution.py:17
  96.3 11.8 %collective-permute-start.26 = (f32[256,128]{1,0:T(8,128)}, f32[256,128]{1,0:T(8,128)S(1)}, u32[]{:S(2)}, u32[]{:S(2)}) collective-permute-start(f32[256,128]{1,0:T(8,128)} %get-tuple-element.15), channel_id=1, source_target_pairs={{0,2},{1,3},{2,0},{3,1},{4,6},{5,7},{6,4},{7,5},{8,10},{9,11},{10,... | collective-permute-start | bytes 393224 | tf_op jit(solution)/shard_map/ppermute | solution.py:17
  97.7 10.4 %collective-permute-start.27 = (f32[256,128]{1,0:T(8,128)}, f32[256,128]{1,0:T(8,128)S(1)}, u32[]{:S(2)}, u32[]{:S(2)}) collective-permute-start(f32[256,128]{1,0:T(8,128)} %get-tuple-element.16), channel_id=1, source_target_pairs={{0,3},{1,2},{2,1},{3,0},{4,7},{5,6},{6,5},{7,4},{8,11},{9,10},{10,... | collective-permute-start | bytes 393224 | tf_op jit(solution)/shard_map/ppermute | solution.py:17
  108.2 7.1 %collective-permute-start.28 = (f32[32,16,128]{2,1,0:T(8,128)S(1)}, f32[32,16,128]{2,1,0:T(8,128)S(1)}, u32[]{:S(2)}, u32[]{:S(2)}) collective-permute-start(f32[32,16,128]{2,1,0:T(8,128)S(1)} %bitcast.152), channel_id=1, source_target_pairs={{0,4},{4,0},{8,12},{12,8},{1,5},{5,1},{9,13},{13,9},{2,6},{6,2},{1... | collective-permute-start | bytes 786440 | tf_op jit(solution)/shard_map/ppermute | solution.py:17
  109.0 6.1 %collective-permute-start.22 = (f32[256,128]{1,0:T(8,128)S(1)}, f32[256,128]{1,0:T(8,128)S(1)}, u32[]{:S(2)}, u32[]{:S(2)}) collective-permute-start(f32[256,128]{1,0:T(8,128)S(1)} %copy-done.38), channel_id=1, source_target_pairs={{0,1},{1,0},{2,3},{3,2},{4,5},{5,4},{6,7},{7,6},{8,9},{9,8},{10,11... | collective-permute-start | bytes 393224 | tf_op jit(solution)/shard_map/ppermute | solution.py:17
  116.1 15.4 %collective-permute-start.29 = (f32[32,16,128]{2,1,0:T(8,128)S(1)}, f32[32,16,128]{2,1,0:T(8,128)S(1)}, u32[]{:S(2)}, u32[]{:S(2)}) collective-permute-start(f32[32,16,128]{2,1,0:T(8,128)S(1)} %fusion.3), channel_id=1, source_target_pairs={{0,8},{4,12},{8,0},{12,4},{1,9},{5,13},{9,1},{13,5},{2,10},{6,14},... | collective-permute-start | bytes 786440 | tf_op jit(solution)/shard_map/ppermute | solution.py:17
  117.6 12.9 %collective-permute-start.24 = (f32[32,16,128]{2,1,0:T(8,128)S(1)}, f32[32,16,128]{2,1,0:T(8,128)S(1)}, u32[]{:S(2)}, u32[]{:S(2)}) collective-permute-start(f32[32,16,128]{2,1,0:T(8,128)S(1)} %fusion.6), channel_id=1, source_target_pairs={{0,8},{4,12},{8,0},{12,4},{1,9},{5,13},{9,1},{13,5},{2,10},{6,14},... | collective-permute-start | bytes 786440 | tf_op jit(solution)/shard_map/ppermute | solution.py:17
  130.9 9.2 %collective-permute-start.25 = (f32[32,16,128]{2,1,0:T(8,128)S(1)}, f32[32,16,128]{2,1,0:T(8,128)S(1)}, u32[]{:S(2)}, u32[]{:S(2)}) collective-permute-start(f32[32,16,128]{2,1,0:T(8,128)S(1)} %fusion.8), channel_id=1, source_target_pairs={{0,16},{16,0},{1,17},{17,1},{2,18},{18,2},{3,19},{19,3},{4,20},{20... | collective-permute-start | bytes 786440 | tf_op jit(solution)/shard_map/ppermute | solution.py:17
  131.9 12.5 %collective-permute-start.30 = (f32[32,16,128]{2,1,0:T(8,128)S(1)}, f32[32,16,128]{2,1,0:T(8,128)S(1)}, u32[]{:S(2)}, u32[]{:S(2)}) collective-permute-start(f32[32,16,128]{2,1,0:T(8,128)S(1)} %fusion.5), channel_id=1, source_target_pairs={{0,16},{16,0},{1,17},{17,1},{2,18},{18,2},{3,19},{19,3},{4,20},{20... | collective-permute-start | bytes 786440 | tf_op jit(solution)/shard_map/ppermute | solution.py:17
  (46 other events, 212.6 us)
